TPU v7x, 512 devices: a whole 4x4x16 slice. The times are simulated.
512 devices in a mesh: slab: 128 (over z_lo, x, y), orb: 4 (over z_hi, core).
Axes of the slice: x: 4, y: 4, z: 16 (z_hi: 2, z_lo: 8; z = z_hi * 8 + z_lo), core: 2. Of those that a mesh axis runs over, the one named last changes fastest.
Arguments:
- orbitals: float32 [4, 512, 256, 512], P('orb', 'slab'), may hold values from -6 to 6
- potential: float32 [512, 256, 512], P('slab'), may hold values from -1 to 1
- coeffs: float32 [3], replicated, may hold values from 0.4 to 1.2
Outputs:
- density: float32 [512, 256, 512], P('slab', 'orb')
All inputs are finite; a program needn't handle non-finite values.
Results may differ from a plain program's by a relative error of at most 0.00002.
Values sent between devices are 32-bit elements; how exact they have to be, the bound alone decides.
A program may use at most 128 MiB of HBM per device.

v0:
```python
import jax
import jax.numpy as jnp
from jax import lax
from jax.sharding import PartitionSpec as P


def extended_2(x, sides, width):
    for axis, dim in sides:
        count, length = (lax.axis_size(axis), x.shape[dim])
        up = [(i, (i + 1) % count) for i in range(count)]
        down = [(j, i) for i, j in up]
        last = lax.slice_in_dim(x, length - width, length, axis=dim)
        leading = lax.slice_in_dim(x, 0, width, axis=dim)
        before = lax.ppermute(last, axis, up)
        after = lax.ppermute(leading, axis, down)
        x = jnp.concatenate([before, x, after], axis=dim)
    return x


def scaled_ext(extended, potential):
    center = extended[2:-2]
    zterm = (
        -2.5 * center
        + 4.0 / 3.0 * (extended[1:-3] + extended[3:-1])
        - 1.0 / 12.0 * (extended[:-4] + extended[4:])
    )
    total = zterm
    for axis in (1, 2):
        near = jnp.roll(center, 1, axis) + jnp.roll(center, -1, axis)
        far = jnp.roll(center, 2, axis) + jnp.roll(center, -2, axis)
        total = total + (-2.5 * center + 4.0 / 3.0 * near - 1.0 / 12.0 * far)
    return (-0.5 * total + potential * center - 4.0 * center) / 5.0


def extend(field):
    return extended_2(field, (("slab", 0),), 2)


def shards(orbitals, potential, coeffs):
    psi = orbitals[0]
    first = scaled_ext(extend(psi), potential)
    second = 2.0 * scaled_ext(extend(first), potential) - psi
    filtered = coeffs[0] * psi + coeffs[1] * first + coeffs[2] * second
    count = lax.axis_size("orb") * orbitals.shape[0]
    term = filtered * filtered / count
    return lax.psum_scatter(term, "orb", scatter_dimension=1, tiled=True)


def solution(mesh):
    return jax.shard_map(
        shards,
        mesh=mesh,
        in_specs=(P("orb", "slab", None, None), P("slab", None, None), P()),
        out_specs=P("slab", "orb", None),
        check_vma=False,
    )
```

profile of v0, /device:TPU:1, one launch (start us, length us, event | category | flops | bytes accessed | tf_op | source)
XLA Modules:
  0.0 216.5 jit_solution(4626026998707257156)
XLA Ops:
  6.5 0.0 copy-start
  6.5 0.0 reduce-scatter.2.cloned.1.call-start
  6.5 1.9 slice_bitcast_fusion.1
  8.4 4.0 %collective-permute-start = (f32[2,256,512]{2,1,0:T(8,128)S(1)}, f32[2,256,512]{2,1,0:T(8,128)S(1)}, u32[]{:S(2)}, u32[]{:S(2)}) collective-permute-start(f32[2,256,512]{2,1,0:T(8,128)S(1)} %get-tuple-element.25), channel_id=1, source_target_pairs={{0,4},{4,8},{8,12},{12,16},{16,20},{20,24},{24,28},{28,32},{32,36}... | collective-permute-start | bytes 3145736 | tf_op jit(solution)/shard_map/ppermute | solution.py:14
  12.4 16.2 %collective-permute-start.1 = (f32[2,256,512]{2,1,0:T(8,128)S(1)}, f32[2,256,512]{2,1,0:T(8,128)S(1)}, u32[]{:S(2)}, u32[]{:S(2)}) collective-permute-start(f32[2,256,512]{2,1,0:T(8,128)S(1)} %get-tuple-element.26), channel_id=1, source_target_pairs={{4,0},{8,4},{12,8},{16,12},{20,16},{24,20},{28,24},{32,28},{36,32}... | collective-permute-start | bytes 3145736 | tf_op jit(solution)/shard_map/ppermute | solution.py:15
  28.7 0.0 copy-done
  28.7 0.2 fusion.61
  28.9 0.5 fusion.60
  29.4 0.0 copy-start.4
  29.5 0.5 fusion.58
  29.9 0.2 copy-done.4
  30.1 0.6 fusion.65
  31.3 1.1 fusion.63
  32.5 2.7 %fusion.64 = (f32[4,256,510]{2,1,0:T(8,128)}, f32[4,256,510]{2,1,0:T(8,128)}) fusion(f32[4,256,512]{2,1,0:T(8,128)S(1)} %bitcast.15), kind=kLoop, calls=%fused_computation.87 | loop fusion | bytes 8355840 | tf_op jit(solution)/shard_map/jit(_roll_static)/slice | solution.py:30
  35.2 0.0 copy-start.1
  35.2 2.8 %fusion.62 = (f32[4,256,511]{2,1,0:T(8,128)}, f32[4,256,511]{2,1,0:T(8,128)}) fusion(f32[4,256,512]{2,1,0:T(8,128)S(1)} %bitcast.16), kind=kLoop, calls=%fused_computation.85 | loop fusion | bytes 8372224 | tf_op jit(solution)/shard_map/jit(_roll_static)/slice | solution.py:29
  38.0 9.3 %collective-permute-done = f32[2,256,512]{2,1,0:T(8,128)S(1)} collective-permute-done((f32[2,256,512]{2,1,0:T(8,128)S(1)}, f32[2,256,512]{2,1,0:T(8,128)S(1)}, u32[]{:S(2)}, u32[]{:S(2)}) %collective-permute-start) | collective-permute-done | bytes 1048608 | tf_op jit(solution)/shard_map/ppermute | solution.py:14
  47.2 0.0 copy-start.2
  47.2 0.9 collective-permute-done.1
  48.1 0.0 copy-start.3
  48.1 0.1 copy-done.2
  48.2 0.9 copy-done.3
  49.1 0.0 copy-done.1
  49.1 8.6 %broadcast_multiply_fusion = (f32[4,256,512]{2,1,0:T(8,128)S(1)}, f32[4,256,512]{2,1,0:T(8,128)}) fusion(f32[4,256,512]{2,1,0:T(8,128)S(1)} %bitcast.17, f32[4,256,512]{2,1,0:T(8,128)S(1)} %copy-done.1, f32[4,256,2]{2,1,0:T(8,128)} %get-tuple-element.40, f32[4,256,510]{2,1,0:T(8,128)} %get-tuple-element.42, f32[4,256,510]{2,1,0:T(8,128)} %get-tuple-element.41, ...), kind=kLoop, calls=%fused_computation.68 | loop fusion | flops 20447232 | bytes 27262976 | tf_op jit(solution)/shard_map/div | solution.py:32
  57.7 1.2 fusion.53
  58.9 0.2 fusion.48
  59.0 0.5 fusion.52
  59.5 0.5 fusion.50
  60.0 1.9 collective-permute-start.2
  61.9 14.9 %collective-permute-start.3 = (f32[2,256,512]{2,1,0:T(8,128)S(1)}, f32[2,256,512]{2,1,0:T(8,128)}, u32[]{:S(2)}, u32[]{:S(2)}) collective-permute-start(f32[2,256,512]{2,1,0:T(8,128)S(1)} %get-tuple-element.8), channel_id=1, source_target_pairs={{4,0},{8,4},{12,8},{16,12},{20,16},{24,20},{28,24},{32,28},{36,32}... | collective-permute-start | bytes 3145736 | tf_op jit(solution)/shard_map/ppermute | solution.py:15
  76.9 1.1 fusion.55
  78.0 2.8 %fusion.54 = (f32[4,256,511]{2,1,0:T(8,128)}, f32[4,256,511]{2,1,0:T(8,128)}) fusion(f32[4,256,512]{2,1,0:T(8,128)S(1)} %get-tuple-element.5), kind=kLoop, calls=%fused_computation.77 | loop fusion | bytes 8372224 | tf_op jit(solution)/shard_map/jit(_roll_static)/slice | solution.py:29
  80.8 2.7 %fusion.56 = (f32[4,256,510]{2,1,0:T(8,128)}, f32[4,256,510]{2,1,0:T(8,128)}) fusion(f32[4,256,512]{2,1,0:T(8,128)S(1)} %get-tuple-element.5), kind=kLoop, calls=%fused_computation.79 | loop fusion | bytes 8355840 | tf_op jit(solution)/shard_map/jit(_roll_static)/slice | solution.py:30
  83.5 11.1 %collective-permute-done.2 = f32[2,256,512]{2,1,0:T(8,128)} collective-permute-done((f32[2,256,512]{2,1,0:T(8,128)S(1)}, f32[2,256,512]{2,1,0:T(8,128)}, u32[]{:S(2)}, u32[]{:S(2)}) %collective-permute-start.2) | collective-permute-done | bytes 1048608 | tf_op jit(solution)/shard_map/ppermute | solution.py:14
  94.6 0.8 collective-permute-done.3
  95.4 11.1 %fusion.46 = f32[4,256,512]{2,1,0:T(8,128)} fusion(f32[4,256,512]{2,1,0:T(8,128)} %get-tuple-element.6, f32[4,256,512]{2,1,0:T(8,128)} %param.4, f32[4,256,512]{2,1,0:T(8,128)S(1)} %get-tuple-element.5, f32[4,256,2]{2,1,0:T(8,128)} %get-tuple-element.22, f32[4,256,510]{2,1,0:T(8,128)} %get-tuple-element.24, f32[4,256,510]{2,1,0:T(8,128)} %get-tuple-element.23, ...), kind=kLoop, calls=%fused_computation.67 | loop fusion | flops 24641536 | bytes 29360140 | tf_op jit(solution)/shard_map/div | solution.py:45
  106.5 0.0 reduce-scatter.2.cloned.1.call-update
  106.6 103.1 %reduce-scatter.2.cloned.1.call-done = f32[4,64,512]{2,1,0:T(8,128)} async-done(((f32[4,256,512]{2,1,0:T(8,128)}), f32[4,64,512]{2,1,0:T(8,128)}) %reduce-scatter.2.cloned.1.call-update) | async-done | bytes 524304 | tf_op jit(solution)/shard_map/reduce_scatter | solution.py:46
  (4 shorter events, 0.1 us)
Async XLA Ops:
  6.5 22.2 %copy-start = (f32[1,4,256,512]{3,2,1,0:T(8,128)S(1)}, f32[1,4,256,512]{3,2,1,0:T(8,128)}, u32[]{:S(2)}) copy-start(f32[1,4,256,512]{3,2,1,0:T(8,128)} %param.3) | copy-start | bytes 6291460
  6.5 203.2 %reduce-scatter.2.cloned.1.call-start = ((), (), s32[]{:S(2)}) async-start(), calls=%async_computation.1 | async-start | bytes 2621440 | tf_op jit(solution)/shard_map/reduce_scatter | solution.py:46
  8.4 38.8 %collective-permute-start = (f32[2,256,512]{2,1,0:T(8,128)S(1)}, f32[2,256,512]{2,1,0:T(8,128)S(1)}, u32[]{:S(2)}, u32[]{:S(2)}) collective-permute-start(f32[2,256,512]{2,1,0:T(8,128)S(1)} %get-tuple-element.25), channel_id=1, source_target_pairs={{0,4},{4,8},{8,12},{12,16},{16,20},{20,24},{24,28},{28,32},{32,36}... | collective-permute-start | bytes 3145736 | tf_op jit(solution)/shard_map/ppermute | solution.py:14
  12.4 35.7 %collective-permute-start.1 = (f32[2,256,512]{2,1,0:T(8,128)S(1)}, f32[2,256,512]{2,1,0:T(8,128)S(1)}, u32[]{:S(2)}, u32[]{:S(2)}) collective-permute-start(f32[2,256,512]{2,1,0:T(8,128)S(1)} %get-tuple-element.26), channel_id=1, source_target_pairs={{4,0},{8,4},{12,8},{16,12},{20,16},{24,20},{28,24},{32,28},{36,32}... | collective-permute-start | bytes 3145736 | tf_op jit(solution)/shard_map/ppermute | solution.py:15
  29.4 0.7 copy-start.4
  35.2 13.9 %copy-start.1 = (f32[4,256,512]{2,1,0:T(8,128)S(1)}, f32[4,256,512]{2,1,0:T(8,128)}, u32[]{:S(2)}) copy-start(f32[4,256,512]{2,1,0:T(8,128)} %param.4) | copy-start | bytes 6291460
  47.2 1.0 copy-start.2
  48.1 1.0 copy-start.3
  60.0 34.6 %collective-permute-start.2 = (f32[2,256,512]{2,1,0:T(8,128)S(1)}, f32[2,256,512]{2,1,0:T(8,128)}, u32[]{:S(2)}, u32[]{:S(2)}) collective-permute-start(f32[2,256,512]{2,1,0:T(8,128)S(1)} %get-tuple-element.7), channel_id=1, source_target_pairs={{0,4},{4,8},{8,12},{12,16},{16,20},{20,24},{24,28},{28,32},{32,36}... | collective-permute-start | bytes 3145736 | tf_op jit(solution)/shard_map/ppermute | solution.py:14
  61.9 33.5 %collective-permute-start.3 = (f32[2,256,512]{2,1,0:T(8,128)S(1)}, f32[2,256,512]{2,1,0:T(8,128)}, u32[]{:S(2)}, u32[]{:S(2)}) collective-permute-start(f32[2,256,512]{2,1,0:T(8,128)S(1)} %get-tuple-element.8), channel_id=1, source_target_pairs={{4,0},{8,4},{12,8},{16,12},{20,16},{24,20},{28,24},{32,28},{36,32}... | collective-permute-start | bytes 3145736 | tf_op jit(solution)/shard_map/ppermute | solution.py:15
Sparse Core Ops, SparseCore 0:
  106.7 102.9 reduce-scatter.1
where the time goes:
time: 217 us
  waiting for transfers between devices  125 us (58%)
  starting transfers between devices  37.1 us (17%)
  local copies, waits for them, and re-layouts  20.4 us (9%)
  other arithmetic  19.7 us (9%)
  between operations  14.2 us (7%)
    reduce_scatter x1, waiting for transfers between devices, shards(): return lax.psum_scatter(term, 'orb', scatter_dimension=1, tiled=True)  103 us
    ppermute x2, starting transfers between devices, extended_2(): after = lax.ppermute(leading, axis, down)  31.2 us
    ppermute x2, waiting for transfers between devices, extended_2(): before = lax.ppermute(last, axis, up)  20.3 us
    div x1, other arithmetic, shards(): term = filtered * filtered / count  11.1 us
    slice x8, local copies, waits for them, and re-layouts, scaled_ext(): far = jnp.roll(center, 2, axis) + jnp.roll(center, -2, axis)  8.69 us
    div x1, other arithmetic, scaled_ext(): return (-0.5 * total + potential * center - 4.0 * center) / 5.0  8.59 us
    slice x8, local copies, waits for them, and re-layouts, scaled_ext(): near = jnp.roll(center, 1, axis) + jnp.roll(center, -1, axis)  7.91 us
    ppermute x2, starting transfers between devices, extended_2(): before = lax.ppermute(last, axis, up)  5.96 us
  transfers between devices with their start and end apart: 5, of which 5 were waited for; matrix products, arithmetic and copies ran while one was open for 7% of the time, Pallas kernels for 0%

commit v1 on v0

v1 whole, which is shorter than its diff:
```python
import jax
import jax.numpy as jnp
from jax import lax
from jax.experimental import pallas as pl
from jax.experimental.pallas import tpu as pltpu
from jax.sharding import PartitionSpec as P

MESH = pl.DeviceIdType.MESH
STEPS = 8
AHEAD = 3


def stencil(cur, prev, nxt, z):
    row = lax.broadcasted_iota(jnp.int32, cur.shape, 0)
    n = cur.shape[1]
    near = pltpu.roll(jnp.where(row == 7, prev, cur), 1, 0) + pltpu.roll(jnp.where(row == 0, nxt, cur), 7, 0)
    far = pltpu.roll(jnp.where(row >= 6, prev, cur), 2, 0) + pltpu.roll(jnp.where(row <= 1, nxt, cur), 6, 0)
    near = near + (pltpu.roll(cur, 1, 1) + pltpu.roll(cur, n - 1, 1)) + (z[1] + z[2])
    far = far + (pltpu.roll(cur, 2, 1) + pltpu.roll(cur, n - 2, 1)) + (z[0] + z[3])
    return far * (1.0 / 120.0) - near * (2.0 / 15.0)


def kernel(
    coef, psi_hbm, pot_hbm, out, psi, pot, first, h1, h2, term, got, zsend, zgot,
    load_sem, s1, r1, s2, r2, cs, cr, zs, zr,
):
    s, o = lax.axis_index("slab"), lax.axis_index("orb")
    count = lax.axis_size("slab")
    core, half = lax.rem(o, 2), o // 2
    up = {"slab": lax.rem(s + 1, count), "orb": o}
    down = {"slab": lax.rem(s + count - 1, count), "orb": o}
    mate = {"slab": s, "orb": o + 1 - 2 * core}
    far_chip = {"slab": s, "orb": lax.rem(o + 2, 4)}

    barrier = pltpu.get_barrier_semaphore()
    for who in (far_chip, up, down, mate):
        pl.semaphore_signal(barrier, inc=1, device_id=who, device_id_type=MESH)
    loads = [
        pltpu.make_async_copy(psi_hbm, psi, load_sem.at[0]),
        pltpu.make_async_copy(pot_hbm, pot, load_sem.at[1]),
    ]
    for copy in loads:
        copy.start()
    pl.semaphore_wait(barrier, 4)

    def halo(src, dst, send, recv, k):
        return [
            pltpu.make_async_remote_copy(
                src_ref=src.at[pl.ds(2, 2), :, k],
                dst_ref=dst.at[0, :, :, k],
                send_sem=send.at[0, k],
                recv_sem=recv.at[0, k],
                device_id=up,
                device_id_type=MESH,
            ),
            pltpu.make_async_remote_copy(
                src_ref=src.at[pl.ds(0, 2), :, k],
                dst_ref=dst.at[1, :, :, k],
                send_sem=send.at[1, k],
                recv_sem=recv.at[1, k],
                device_id=down,
                device_id_type=MESH,
            ),
        ]

    one = [halo(psi_hbm, h1, s1, r1, k) for k in range(STEPS)]
    two = [halo(first, h2, s2, r2, k) for k in range(STEPS)]
    to_mate = [
        pltpu.make_async_remote_copy(
            src_ref=term.at[1 - core, :, :, k],
            dst_ref=got.at[:, :, k],
            send_sem=cs.at[k],
            recv_sem=cr.at[k],
            device_id=mate,
            device_id_type=MESH,
        )
        for k in range(STEPS)
    ]
    to_far = [
        pltpu.make_async_remote_copy(
            src_ref=zsend.at[:, k],
            dst_ref=zgot.at[:, k],
            send_sem=zs.at[k],
            recv_sem=zr.at[k],
            device_id=far_chip,
            device_id_type=MESH,
        )
        for k in range(STEPS)
    ]

    def start(copies):
        for copy in copies:
            copy.start()

    def received(copies):
        for copy in copies:
            copy.wait_recv()

    def tiles(own, halos, j, k):
        flat = j * STEPS + k
        before, after = lax.rem(flat + 31, 32), lax.rem(flat + 1, 32)
        planes = [halos[0, 0, j, k], halos[0, 1, j, k]]
        planes += [own[p, j, k] for p in range(4)]
        planes += [halos[1, 0, j, k], halos[1, 1, j, k]]
        for p in range(4):
            prev = own[p, before // STEPS, lax.rem(before, STEPS)]
            nxt = own[p, after // STEPS, lax.rem(after, STEPS)]
            z = (planes[p], planes[p + 1], planes[p + 3], planes[p + 4])
            yield p, planes[p + 2], stencil(planes[p + 2], prev, nxt, z)

    def first_step(k):
        def body(j, carry):
            for p, cur, rest in tiles(psi, h1, j, k):
                first[p, j, k] = cur * (pot[p, j, k] * 0.2 - 0.05) + rest
            return carry

        lax.fori_loop(0, 4, body, 0)

    a = 0.5 * (coef[0] - coef[2])
    b = 0.5 * coef[1]
    d = coef[2]

    def second_step(k):
        def body(j, carry):
            for p, cur, rest in tiles(first, h2, j, k):
                scaled = cur * (pot[p, j, k] * 0.2 - 0.05) + rest
                value = a * psi[p, j, k] + b * cur + d * scaled
                term[lax.rem(j, 2), j // 2, p, k] = value * value
            return carry

        lax.fori_loop(0, 4, body, 0)
        to_mate[k].start()

    def far_step(k):
        to_mate[k].wait_recv()
        for p in range(4):
            zsend[p, k] = term[core, 1 - half, p, k] + got[1 - half, p, k]
        to_far[k].start()

    def last_step(k):
        to_far[k].wait_recv()
        for p in range(4):
            out[p, k] = (term[core, half, p, k] + got[half, p, k]) + zgot[p, k]

    for k in range(AHEAD):
        start(one[k])
    for copy in loads:
        copy.wait()
    order = [*range(1, STEPS), 0]
    for k in range(STEPS):
        received(one[k])
        first_step(k)
        if k >= 1:
            start(two[k])
        if k + AHEAD < STEPS:
            start(one[k + AHEAD])
        if k == STEPS - 1:
            start(two[0])
        if k >= 3:
            far_step(k - 2)
        if k >= 2:
            received(two[k - 1])
            second_step(k - 1)
    far_step(STEPS - 2)
    received(two[STEPS - 1])
    second_step(STEPS - 1)
    far_step(STEPS - 1)
    received(two[0])
    second_step(0)
    far_step(0)
    for k in order:
        last_step(k)
    for k in range(STEPS):
        for copy in (*one[k], *two[k], to_mate[k], to_far[k]):
            copy.wait_send()


def shards(orbitals, potential, coeffs):
    planes, rows, width = potential.shape
    grid = (planes, 4, STEPS, rows // (4 * STEPS), width)
    tile = grid[3:]
    halos = pltpu.VMEM((2, 2, 4, STEPS, *tile), jnp.float32)
    whole = pltpu.VMEM(grid, jnp.float32)
    quarter = (planes, STEPS, *tile)
    dma = pltpu.SemaphoreType.DMA
    out = pl.pallas_call(
        kernel,
        out_shape=jax.ShapeDtypeStruct(quarter, jnp.float32),
        in_specs=[
            pl.BlockSpec(memory_space=pltpu.SMEM),
            pl.BlockSpec(memory_space=pl.ANY),
            pl.BlockSpec(memory_space=pl.ANY),
        ],
        out_specs=pl.BlockSpec(memory_space=pltpu.VMEM),
        scratch_shapes=[
            whole, whole, whole, halos, halos,
            pltpu.VMEM((2, 2, *quarter), jnp.float32),
            pltpu.VMEM((2, *quarter), jnp.float32),
            pltpu.VMEM(quarter, jnp.float32),
            pltpu.VMEM(quarter, jnp.float32),
            dma((2,)),
            dma((2, STEPS)), dma((2, STEPS)), dma((2, STEPS)), dma((2, STEPS)),
            dma((STEPS,)), dma((STEPS,)), dma((STEPS,)), dma((STEPS,)),
        ],
        compiler_params=pltpu.CompilerParams(collective_id=0, has_side_effects=True),
        name="filter_density",
    )(coeffs, orbitals.reshape(grid), potential.reshape(grid))
    return out.reshape(planes, rows // 4, width)


def solution(mesh):
    return jax.shard_map(
        shards,
        mesh=mesh,
        in_specs=(P("orb", "slab", None, None), P("slab", None, None), P()),
        out_specs=P("slab", "orb", None),
        check_vma=False,
    )
```

time: 217 us -> 125 us (0.58)
  waiting for transfers between devices: 125 us -> 0 us
  Pallas kernels: 0 us -> 123 us
  starting transfers between devices: 37.1 us -> 0 us
  other arithmetic: 19.7 us -> 0 us
  local copies, waits for them, and re-layouts: 20.4 us -> 1.87 us
  between operations: 14.2 us -> 0.01 us
    pallas_call x0 -> x1, Pallas kernels: none -> 123 us  [shards(): pl.pallas_call(kernel, out_shape=jax.ShapeDtypeStruct(quarter, jnp.float3...]
    reduce_scatter x1 -> x0, waiting for transfers between devices: 103 us -> none  [shards(): return lax.psum_scatter(term, 'orb', scatter_dimension=1, tiled=True)]
    ppermute x4 -> x0, starting transfers between devices: 37.1 us -> none  [the longest x2 31.2 us: extended_2(): after = lax.ppermute(leading, axis, down)]
    ppermute x4 -> x0, waiting for transfers between devices: 22 us -> none  [the longest x2 20.3 us: extended_2(): before = lax.ppermute(last, axis, up)]
    div x2 -> x0, other arithmetic: 19.7 us -> none  [the longest x1 11.1 us: shards(): term = filtered * filtered / count]
    slice x19 -> x0, local copies, waits for them, and re-layouts: 19.2 us -> none  [the longest x8 8.69 us: scaled_ext(): far = jnp.roll(center, 2, axis) + jnp.roll(center, -2, axis)]
  transfers between devices with their start and end apart: 5 -> 0, of which waited for: 5 -> 0; matrix products, arithmetic and copies ran while one was open for 7% -> 0% of each run, Pallas kernels for 0% -> 0%
where the time goes in v1:
time: 125 us
  Pallas kernels  123 us (98%)
  local copies, waits for them, and re-layouts  1.87 us (1%)
    pallas_call x1, Pallas kernels, shards(): pl.pallas_call(kernel, out_shape=jax.ShapeDtypeStruct(quarter, jnp.float3...  123 us

profile of v1, /device:TPU:1, one launch (start us, length us, event | category | flops | bytes accessed | tf_op | source)
XLA Modules:
  0.0 125.0 jit_solution(13815901423497052069)
XLA Ops:
  0.0 123.1 %filter_density.1 = f32[4,8,8,512]{3,2,1,0:T(8,128)} custom-call(f32[3]{0:T(128)} %coef.1, f32[4,4,8,8,512]{4,3,2,1,0:T(8,128)} %bitcast.3, f32[4,4,8,8,512]{4,3,2,1,0:T(8,128)} %bitcast.4), custom_call_target="tpu_custom_call" | custom-call | tf_op jit(solution)/shard_map/filter_density/pallas_call | solution.py:186
  123.1 1.9 %copy.5 = f32[4,64,512]{2,1,0:T(8,128)} copy(f32[4,64,512]{2,1,0:T(8,128)} %bitcast.5) | data formatting | bytes 1048576

commit v2 on v1

--- a/solution.py
+++ b/solution.py
@@ -21,8 +21,8 @@
 
 
 def kernel(
-    coef, psi_hbm, pot_hbm, out, psi, pot, first, h1, h2, term, got, zsend, zgot,
-    load_sem, s1, r1, s2, r2, cs, cr, zs, zr,
+    coef, psi_hbm, pot_hbm, out, psi, pot, first, h1, h2, term, got, zsend, zgot, passing,
+    load_sem, s1, r1, s2, r2, cs, cr, zs, zr, pass_in, pass_out,
 ):
     s, o = lax.axis_index("slab"), lax.axis_index("orb")
     count = lax.axis_size("slab")
@@ -32,7 +32,25 @@
     mate = {"slab": s, "orb": o + 1 - 2 * core}
     far_chip = {"slab": s, "orb": lax.rem(o + 2, 4)}
 
+    xy = lax.rem(s, 16)
+    group = xy // 8
+    turn = xy + group * (15 - 2 * xy)
+    edge = s - xy + 15 * group
+
+    def by(k, half_of=None):
+        return {"slab": s - xy + k + group * (15 - 2 * k), "orb": o if half_of is None else half_of}
+
     barrier = pltpu.get_barrier_semaphore()
+
+    @pl.when(turn == 0)
+    def _():
+        for k in range(1, STEPS):
+            pl.semaphore_signal(barrier, inc=1, device_id=by(k, lax.rem(o + 2, 4)), device_id_type=MESH)
+
+    @pl.when(turn != 0)
+    def _():
+        pl.semaphore_signal(barrier, inc=1, device_id={"slab": edge, "orb": o}, device_id_type=MESH)
+
     for who in (far_chip, up, down, mate):
         pl.semaphore_signal(barrier, inc=1, device_id=who, device_id_type=MESH)
     loads = [
@@ -41,7 +59,14 @@
     ]
     for copy in loads:
         copy.start()
-    pl.semaphore_wait(barrier, 4)
+
+    @pl.when(turn == 0)
+    def _():
+        pl.semaphore_wait(barrier, 4 + STEPS - 1)
+
+    @pl.when(turn != 0)
+    def _():
+        pl.semaphore_wait(barrier, 5)
 
     def halo(src, dst, send, recv, k):
         return [
@@ -88,6 +113,18 @@
         for k in range(STEPS)
     ]
 
+    to_pass = [
+        pltpu.make_async_remote_copy(
+            src_ref=zsend.at[:, k],
+            dst_ref=passing,
+            send_sem=zs.at[k],
+            recv_sem=pass_in.at[0],
+            device_id=by(k),
+            device_id_type=MESH,
+        )
+        for k in range(STEPS)
+    ]
+
     def start(copies):
         for copy in copies:
             copy.start()
@@ -135,7 +172,26 @@
         to_mate[k].wait_recv()
         for p in range(4):
             zsend[p, k] = term[core, 1 - half, p, k] + got[1 - half, p, k]
-        to_far[k].start()
+        if k == 0:
+            to_far[k].start()
+        else:
+            pl.when(turn == 0)(to_pass[k].start)
+            pl.when(turn != 0)(to_far[k].start)
+
+    def pass_on(k):
+        @pl.when(turn == k)
+        def _():
+            to_pass[k].wait_recv()
+            copy = pltpu.make_async_remote_copy(
+                src_ref=passing,
+                dst_ref=zgot.at[:, k],
+                send_sem=pass_out.at[0],
+                recv_sem=zr.at[k],
+                device_id={"slab": edge, "orb": lax.rem(o + 2, 4)},
+                device_id_type=MESH,
+            )
+            copy.start()
+            copy.wait_send()
 
     def last_step(k):
         to_far[k].wait_recv()
@@ -161,6 +217,8 @@
         if k >= 2:
             received(two[k - 1])
             second_step(k - 1)
+        if k >= STEPS - 2:
+            pass_on(k - STEPS + 3)
     far_step(STEPS - 2)
     received(two[STEPS - 1])
     second_step(STEPS - 1)
@@ -168,6 +226,8 @@
     received(two[0])
     second_step(0)
     far_step(0)
+    for k in range(3, STEPS):
+        pass_on(k)
     for k in order:
         last_step(k)
     for k in range(STEPS):
@@ -198,9 +258,10 @@
             pltpu.VMEM((2, *quarter), jnp.float32),
             pltpu.VMEM(quarter, jnp.float32),
             pltpu.VMEM(quarter, jnp.float32),
+            pltpu.VMEM((planes, *tile), jnp.float32),
             dma((2,)),
             dma((2, STEPS)), dma((2, STEPS)), dma((2, STEPS)), dma((2, STEPS)),
-            dma((STEPS,)), dma((STEPS,)), dma((STEPS,)), dma((STEPS,)),
+            dma((STEPS,)), dma((STEPS,)), dma((STEPS,)), dma((STEPS,)), dma((1,)), dma((1,)),
         ],
         compiler_params=pltpu.CompilerParams(collective_id=0, has_side_effects=True),
         name="filter_density",

time: 125 us -> 104 us (0.83)
  Pallas kernels: 123 us -> 102 us
    pallas_call x1, Pallas kernels: 123 us -> 102 us  [shards(): pl.pallas_call(kernel, out_shape=jax.ShapeDtypeStruct(quarter, jnp.float3...]
where the time goes in v2:
time: 104 us
  Pallas kernels  102 us (98%)
  local copies, waits for them, and re-layouts  1.87 us (2%)
    pallas_call x1, Pallas kernels, shards(): pl.pallas_call(kernel, out_shape=jax.ShapeDtypeStruct(quarter, jnp.float3...  102 us

profile of v2, /device:TPU:1, one launch (start us, length us, event | category | flops | bytes accessed | tf_op | source)
XLA Modules:
  0.0 104.0 jit_solution(9953213255623112344)
XLA Ops:
  0.0 102.1 %filter_density.1 = f32[4,8,8,512]{3,2,1,0:T(8,128)} custom-call(f32[3]{0:T(128)} %coef.1, f32[4,4,8,8,512]{4,3,2,1,0:T(8,128)} %bitcast.3, f32[4,4,8,8,512]{4,3,2,1,0:T(8,128)} %bitcast.4), custom_call_target="tpu_custom_call" | custom-call | tf_op jit(solution)/shard_map/filter_density/pallas_call | solution.py:246
  102.1 1.9 %copy.5 = f32[4,64,512]{2,1,0:T(8,128)} copy(f32[4,64,512]{2,1,0:T(8,128)} %bitcast.5) | data formatting | bytes 1048576

commit v3 on v1

v3 whole, which is shorter than its diff:
```python
import jax
import jax.numpy as jnp
from jax import lax
from jax.experimental import pallas as pl
from jax.experimental.pallas import tpu as pltpu
from jax.sharding import PartitionSpec as P

MESH = pl.DeviceIdType.MESH
STEPS = 16
TURNS = STEPS // 2
AHEAD, AHEAD_TURN, AHEAD_WRAP = 4, 4, 10
LAG, LAG_TURN, LAG_WRAP = 1, 1, 4
PASS = 8


def stencil(cur, prev, nxt, z):
    row = lax.broadcasted_iota(jnp.int32, cur.shape, 0)
    n = cur.shape[1]
    near = pltpu.roll(jnp.where(row == 7, prev, cur), 1, 0) + pltpu.roll(jnp.where(row == 0, nxt, cur), 7, 0)
    far = pltpu.roll(jnp.where(row >= 6, prev, cur), 2, 0) + pltpu.roll(jnp.where(row <= 1, nxt, cur), 6, 0)
    near = near + (pltpu.roll(cur, 1, 1) + pltpu.roll(cur, n - 1, 1)) + (z[1] + z[2])
    far = far + (pltpu.roll(cur, 2, 1) + pltpu.roll(cur, n - 2, 1)) + (z[0] + z[3])
    return far * (1.0 / 120.0) - near * (2.0 / 15.0)


def kernel(
    coef, psi_hbm, pot_hbm, out, psi, pot, first, h1, h2, term, got, zsend, zgot, passing,
    load_sem, s1, r1, s2, r2, cs, cr, zs, zr, pass_in, pass_out,
):
    s, o = lax.axis_index("slab"), lax.axis_index("orb")
    count = lax.axis_size("slab")
    core, half = lax.rem(o, 2), o // 2
    up = {"slab": lax.rem(s + 1, count), "orb": o}
    down = {"slab": lax.rem(s + count - 1, count), "orb": o}
    mate = {"slab": s, "orb": o + 1 - 2 * core}
    far_chip = {"slab": s, "orb": lax.rem(o + 2, 4)}

    xy = lax.rem(s, 16)
    group = xy // 8
    turn = xy + group * (15 - 2 * xy)
    edge = s - xy + 15 * group

    def by(k, half_of=None):
        return {"slab": s - xy + k + group * (15 - 2 * k), "orb": o if half_of is None else half_of}

    barrier = pltpu.get_barrier_semaphore()

    @pl.when(turn == 0)
    def _():
        for k in range(1, TURNS):
            pl.semaphore_signal(barrier, inc=1, device_id=by(k, lax.rem(o + 2, 4)), device_id_type=MESH)

    @pl.when(turn != 0)
    def _():
        pl.semaphore_signal(barrier, inc=1, device_id={"slab": edge, "orb": o}, device_id_type=MESH)

    for who in (far_chip, up, down, mate):
        pl.semaphore_signal(barrier, inc=1, device_id=who, device_id_type=MESH)
    loads = [
        pltpu.make_async_copy(psi_hbm, psi, load_sem.at[0]),
        pltpu.make_async_copy(pot_hbm, pot, load_sem.at[1]),
    ]
    for copy in loads:
        copy.start()

    @pl.when(turn == 0)
    def _():
        pl.semaphore_wait(barrier, 4 + TURNS - 1)

    @pl.when(turn != 0)
    def _():
        pl.semaphore_wait(barrier, 5)

    def halo(src, dst, send, recv, k):
        return [
            pltpu.make_async_remote_copy(
                src_ref=src.at[pl.ds(2, 2), :, k],
                dst_ref=dst.at[0, :, :, k],
                send_sem=send.at[0, k],
                recv_sem=recv.at[0, k],
                device_id=up,
                device_id_type=MESH,
            ),
            pltpu.make_async_remote_copy(
                src_ref=src.at[pl.ds(0, 2), :, k],
                dst_ref=dst.at[1, :, :, k],
                send_sem=send.at[1, k],
                recv_sem=recv.at[1, k],
                device_id=down,
                device_id_type=MESH,
            ),
        ]

    def one(k):
        return halo(psi_hbm, h1, s1, r1, k)

    def two(k):
        return halo(first, h2, s2, r2, k)

    def to_mate(r):
        return pltpu.make_async_remote_copy(
            src_ref=term.at[1 - core, :, :, r],
            dst_ref=got.at[:, :, r],
            send_sem=cs.at[r],
            recv_sem=cr.at[r],
            device_id=mate,
            device_id_type=MESH,
        )

    def to_far(r):
        return pltpu.make_async_remote_copy(
            src_ref=zsend.at[:, r],
            dst_ref=zgot.at[:, r],
            send_sem=zs.at[r],
            recv_sem=zr.at[r],
            device_id=far_chip,
            device_id_type=MESH,
        )

    def to_pass(r, column):
        return pltpu.make_async_remote_copy(
            src_ref=zsend.at[:, r],
            dst_ref=passing,
            send_sem=zs.at[r],
            recv_sem=pass_in.at[0],
            device_id=by(column),
            device_id_type=MESH,
        )

    def start(copies):
        for copy in copies:
            copy.start()

    def received(copies):
        for copy in copies:
            copy.wait_recv()

    def tiles(own, halos, j, k):
        flat = j * STEPS + k
        before, after = lax.rem(flat + 2 * STEPS - 1, 2 * STEPS), lax.rem(flat + 1, 2 * STEPS)
        planes = [halos[0, 0, j, k], halos[0, 1, j, k]]
        planes += [own[p, j, k] for p in range(4)]
        planes += [halos[1, 0, j, k], halos[1, 1, j, k]]
        for p in range(4):
            prev = own[p, before // STEPS, lax.rem(before, STEPS)]
            nxt = own[p, after // STEPS, lax.rem(after, STEPS)]
            z = (planes[p], planes[p + 1], planes[p + 3], planes[p + 4])
            yield p, planes[p + 2], stencil(planes[p + 2], prev, nxt, z)

    def first_step(k):
        def body(j, carry):
            for p, cur, rest in tiles(psi, h1, j, k):
                first[p, j, k] = cur * (pot[p, j, k] * 0.2 - 0.05) + rest
            return carry

        lax.fori_loop(0, 2, body, 0)

    a = 0.5 * (coef[0] - coef[2])
    b = 0.5 * coef[1]
    d = coef[2]

    def second_step(k):
        owner, r = k // TURNS, lax.rem(k, TURNS)

        def body(j, carry):
            for p, cur, rest in tiles(first, h2, j, k):
                scaled = cur * (pot[p, j, k] * 0.2 - 0.05) + rest
                value = a * psi[p, j, k] + b * cur + d * scaled
                term[owner, j, p, r] = value * value
            return carry

        lax.fori_loop(0, 2, body, 0)

        @pl.when(core != owner)
        def _():
            to_mate(r).start()

    def far_step(k):
        owner, r = k // TURNS, lax.rem(k, TURNS)

        @pl.when(core == owner)
        def _():
            to_mate(r).wait_recv()
            for p in range(4):
                zsend[p, r] = term[owner, 1 - half, p, r] + got[1 - half, p, r]
            column = lax.rem(r + core, TURNS)
            passes = jnp.logical_and(turn == 0, column != 0)

            @pl.when(passes)
            def _():
                to_pass(r, column).start()

            @pl.when(jnp.logical_not(passes))
            def _():
                to_far(r).start()

    def pass_on():
        to_pass(pass_row, turn).wait_recv()
        copy = pltpu.make_async_remote_copy(
            src_ref=passing,
            dst_ref=zgot.at[:, pass_row],
            send_sem=pass_out.at[0],
            recv_sem=zr.at[pass_row],
            device_id={"slab": edge, "orb": lax.rem(o + 2, 4)},
            device_id_type=MESH,
        )
        copy.start()
        copy.wait_send()

    def each(first_k, last_k, body):
        def step(k, carry):
            body(k)
            return carry

        lax.fori_loop(first_k, last_k, step, 0)

    def wraps(slab, width):
        return lax.rem(slab + width, count) // (2 * width) == 0

    turns = lax.rem(s + 1, 4) // 2 == 0
    ahead = jnp.where(wraps(s, 1), AHEAD_WRAP, jnp.where(turns, AHEAD_TURN, AHEAD))
    lag = jnp.where(wraps(s, 2), LAG_WRAP, jnp.where(turns, LAG_TURN, LAG))
    pass_row = lax.rem(turn - core + TURNS, TURNS)
    pass_slot = core * TURNS + pass_row + jnp.where(wraps(edge, 1), LAG_WRAP, LAG_TURN) + PASS

    each(0, ahead, lambda k: start(one(k)))
    for copy in loads:
        copy.wait()

    def slot(t):
        @pl.when(t < STEPS)
        def _():
            received(one(t))
            first_step(t)

            @pl.when(t > 0)
            def _():
                start(two(t))

            @pl.when(t + ahead < STEPS)
            def _():
                start(one(t + ahead))

            @pl.when(t == STEPS - 1)
            def _():
                start(two(0))

        m = t - lag

        @pl.when(jnp.logical_and(m > 1, m < STEPS + 2))
        def _():
            far_step(lax.rem(m - 1, STEPS))

        @pl.when(jnp.logical_and(m > 0, m < STEPS + 1))
        def _():
            k = lax.rem(m, STEPS)
            received(two(k))
            second_step(k)

        @pl.when(jnp.logical_and(t == pass_slot, turn != 0))
        def _():
            pass_on()

    each(0, STEPS + 2 + LAG_WRAP + PASS, slot)

    def last_step(r):
        to_far(r).wait_recv()
        for p in range(4):
            out[p, r] = (term[core, half, p, r] + got[half, p, r]) + zgot[p, r]

    each(0, TURNS, last_step)

    def sent(k):
        for copy in (*one(k), *two(k)):
            copy.wait_send()

    each(0, STEPS, sent)

    def sums_sent(r):
        to_mate(r).wait_send()
        to_far(r).wait_send()

    each(0, TURNS, sums_sent)


def shards(orbitals, potential, coeffs):
    planes, rows, width = potential.shape
    grid = (planes, 2, STEPS, rows // (2 * STEPS), width)
    tile = grid[3:]
    halos = pltpu.VMEM((2, 2, 2, STEPS, *tile), jnp.float32)
    whole = pltpu.VMEM(grid, jnp.float32)
    quarter = (planes, TURNS, *tile)
    dma = pltpu.SemaphoreType.DMA
    out = pl.pallas_call(
        kernel,
        out_shape=jax.ShapeDtypeStruct(quarter, jnp.float32),
        in_specs=[
            pl.BlockSpec(memory_space=pltpu.SMEM),
            pl.BlockSpec(memory_space=pl.ANY),
            pl.BlockSpec(memory_space=pl.ANY),
        ],
        out_specs=pl.BlockSpec(memory_space=pltpu.VMEM),
        scratch_shapes=[
            whole, whole, whole, halos, halos,
            pltpu.VMEM((2, 2, *quarter), jnp.float32),
            pltpu.VMEM((2, *quarter), jnp.float32),
            pltpu.VMEM(quarter, jnp.float32),
            pltpu.VMEM(quarter, jnp.float32),
            pltpu.VMEM((planes, *tile), jnp.float32),
            dma((2,)),
            dma((2, STEPS)), dma((2, STEPS)), dma((2, STEPS)), dma((2, STEPS)),
            dma((TURNS,)), dma((TURNS,)), dma((TURNS,)), dma((TURNS,)), dma((1,)), dma((1,)),
        ],
        compiler_params=pltpu.CompilerParams(collective_id=0, has_side_effects=True),
        name="filter_density",
    )(coeffs, orbitals.reshape(grid), potential.reshape(grid))
    return out.reshape(planes, rows // 4, width)


def solution(mesh):
    return jax.shard_map(
        shards,
        mesh=mesh,
        in_specs=(P("orb", "slab", None, None), P("slab", None, None), P()),
        out_specs=P("slab", "orb", None),
        check_vma=False,
    )
```

time: 125 us -> 94.9 us (0.76)
  Pallas kernels: 123 us -> 92.7 us
    pallas_call x1, Pallas kernels: 123 us -> 92.7 us  [shards(): pl.pallas_call(kernel, out_shape=jax.ShapeDtypeStruct(quarter, jnp.float3...]
where the time goes in v3:
time: 94.9 us; the launch traced here: 94.5 us
  Pallas kernels  92.7 us (98%)
  local copies, waits for them, and re-layouts  1.87 us (2%)
    pallas_call x1, Pallas kernels, shards(): pl.pallas_call(kernel, out_shape=jax.ShapeDtypeStruct(quarter, jnp.float3...  92.7 us

profile of v3, /device:TPU:1, one launch (start us, length us, event | category | flops | bytes accessed | tf_op | source)
XLA Modules:
  0.0 94.5 jit_solution(12871861694922839625)
XLA Ops:
  0.0 92.7 %filter_density.1 = f32[4,8,8,512]{3,2,1,0:T(8,128)} custom-call(f32[3]{0:T(128)} %coef.1, f32[4,2,16,8,512]{4,3,2,1,0:T(8,128)} %bitcast.3, f32[4,2,16,8,512]{4,3,2,1,0:T(8,128)} %bitcast.4), custom_call_target="tpu_custom_call" | custom-call | tf_op jit(solution)/shard_map/filter_density/pallas_call | solution.py:294
  92.7 1.9 %copy.5 = f32[4,64,512]{2,1,0:T(8,128)} copy(f32[4,64,512]{2,1,0:T(8,128)} %bitcast.5) | data formatting | bytes 1048576

commit v4 on v3

--- a/solution.py
+++ b/solution.py
@@ -8,8 +8,9 @@
 MESH = pl.DeviceIdType.MESH
 STEPS = 16
 TURNS = STEPS // 2
-AHEAD, AHEAD_TURN, AHEAD_WRAP = 4, 4, 10
-LAG, LAG_TURN, LAG_WRAP = 1, 1, 4
+AHEAD = (4, 4, 5, 5, 10)
+LAG = (1, 1, 2, 4, 4)
+DIRECT = 2
 PASS = 8
 
 
@@ -92,10 +93,10 @@
         ]
 
     def one(k):
-        return halo(psi_hbm, h1, s1, r1, k)
+        return halo(psi_hbm, h1, s1, r1, STEPS - 1 - k)
 
     def two(k):
-        return halo(first, h2, s2, r2, k)
+        return halo(first, h2, s2, r2, STEPS - 1 - k)
 
     def to_mate(r):
         return pltpu.make_async_remote_copy(
@@ -147,7 +148,9 @@
             z = (planes[p], planes[p + 1], planes[p + 3], planes[p + 4])
             yield p, planes[p + 2], stencil(planes[p + 2], prev, nxt, z)
 
-    def first_step(k):
+    def first_step(step):
+        k = STEPS - 1 - step
+
         def body(j, carry):
             for p, cur, rest in tiles(psi, h1, j, k):
                 first[p, j, k] = cur * (pot[p, j, k] * 0.2 - 0.05) + rest
@@ -159,7 +162,8 @@
     b = 0.5 * coef[1]
     d = coef[2]
 
-    def second_step(k):
+    def second_step(step):
+        k = STEPS - 1 - step
         owner, r = k // TURNS, lax.rem(k, TURNS)
 
         def body(j, carry):
@@ -175,7 +179,8 @@
         def _():
             to_mate(r).start()
 
-    def far_step(k):
+    def far_step(step):
+        k = STEPS - 1 - step
         owner, r = k // TURNS, lax.rem(k, TURNS)
 
         @pl.when(core == owner)
@@ -184,7 +189,7 @@
             for p in range(4):
                 zsend[p, r] = term[owner, 1 - half, p, r] + got[1 - half, p, r]
             column = lax.rem(r + core, TURNS)
-            passes = jnp.logical_and(turn == 0, column != 0)
+            passes = jnp.logical_and(turn == 0, column >= DIRECT)
 
             @pl.when(passes)
             def _():
@@ -217,11 +222,15 @@
     def wraps(slab, width):
         return lax.rem(slab + width, count) // (2 * width) == 0
 
-    turns = lax.rem(s + 1, 4) // 2 == 0
-    ahead = jnp.where(wraps(s, 1), AHEAD_WRAP, jnp.where(turns, AHEAD_TURN, AHEAD))
-    lag = jnp.where(wraps(s, 2), LAG_WRAP, jnp.where(turns, LAG_TURN, LAG))
+    def pick(table, slab):
+        value = jnp.where(lax.rem(slab + 1, 4) // 2 == 0, table[1], table[0])
+        value = jnp.where(lax.rem(slab + 1, 16) // 2 == 0, table[2], value)
+        value = jnp.where(wraps(slab, 2), table[3], value)
+        return jnp.where(wraps(slab, 1), table[4], value)
+
+    ahead, lag = pick(AHEAD, s), pick(LAG, s)
     pass_row = lax.rem(turn - core + TURNS, TURNS)
-    pass_slot = core * TURNS + pass_row + jnp.where(wraps(edge, 1), LAG_WRAP, LAG_TURN) + PASS
+    pass_slot = STEPS - 1 - core * TURNS - pass_row + pick(LAG, edge) + PASS
 
     each(0, ahead, lambda k: start(one(k)))
     for copy in loads:
@@ -257,11 +266,11 @@
             received(two(k))
             second_step(k)
 
-        @pl.when(jnp.logical_and(t == pass_slot, turn != 0))
+        @pl.when(jnp.logical_and(t == pass_slot, turn >= DIRECT))
         def _():
             pass_on()
 
-    each(0, STEPS + 2 + LAG_WRAP + PASS, slot)
+    each(0, STEPS + 2 + max(LAG) + PASS, slot)
 
     def last_step(r):
         to_far(r).wait_recv()

time: 94.9 us -> 92.9 us (0.979)
  Pallas kernels: 92.7 us -> 90.8 us
    pallas_call x1, Pallas kernels: 92.7 us -> 90.8 us  [shards(): pl.pallas_call(kernel, out_shape=jax.ShapeDtypeStruct(quarter, jnp.float3...]
where the time goes in v4:
time: 92.9 us; the launch traced here: 92.7 us
  Pallas kernels  90.8 us (98%)
  local copies, waits for them, and re-layouts  1.87 us (2%)
    pallas_call x1, Pallas kernels, shards(): pl.pallas_call(kernel, out_shape=jax.ShapeDtypeStruct(quarter, jnp.float3...  90.8 us
    unnamed x1, local copies, waits for them, and re-layouts  1.87 us

profile of v4, /device:TPU:1, one launch (start us, length us, event | category | flops | bytes accessed | tf_op | source)
XLA Modules:
  0.0 92.7 jit_solution(13714397061028783461)
XLA Ops:
  0.0 90.8 %filter_density.1 = f32[4,8,8,512]{3,2,1,0:T(8,128)} custom-call(f32[3]{0:T(128)} %coef.1, f32[4,2,16,8,512]{4,3,2,1,0:T(8,128)} %bitcast.3, f32[4,2,16,8,512]{4,3,2,1,0:T(8,128)} %bitcast.4), custom_call_target="tpu_custom_call" | custom-call | tf_op jit(solution)/shard_map/filter_density/pallas_call | solution.py:303
  90.8 1.9 %copy.5 = f32[4,64,512]{2,1,0:T(8,128)} copy(f32[4,64,512]{2,1,0:T(8,128)} %bitcast.5) | data formatting | bytes 1048576

commit v5 on v4

--- a/solution.py
+++ b/solution.py
@@ -9,9 +9,9 @@
 STEPS = 16
 TURNS = STEPS // 2
 AHEAD = (4, 4, 5, 5, 10)
-LAG = (1, 1, 2, 4, 4)
+LAG = (1, 2, 2, 4, 5)
 DIRECT = 2
-PASS = 8
+PASS = 6
 
 
 def stencil(cur, prev, nxt, z):
@@ -25,7 +25,7 @@
 
 
 def kernel(
-    coef, psi_hbm, pot_hbm, out, psi, pot, first, h1, h2, term, got, zsend, zgot, passing,
+    coef, psi_hbm, pot_hbm, mine_hbm, zgot, psi, pot, first, h1, h2, term, got, zsend, mine, passing,
     load_sem, s1, r1, s2, r2, cs, cr, zs, zr, pass_in, pass_out,
 ):
     s, o = lax.axis_index("slab"), lax.axis_index("orb")
@@ -158,9 +158,9 @@
 
         lax.fori_loop(0, 2, body, 0)
 
-    a = 0.5 * (coef[0] - coef[2])
-    b = 0.5 * coef[1]
-    d = coef[2]
+    a = coef[0] - coef[2]
+    b = coef[1]
+    d = 2.0 * coef[2]
 
     def second_step(step):
         k = STEPS - 1 - step
@@ -272,12 +272,15 @@
 
     each(0, STEPS + 2 + max(LAG) + PASS, slot)
 
-    def last_step(r):
-        to_far(r).wait_recv()
+    def own_sums(r):
         for p in range(4):
-            out[p, r] = (term[core, half, p, r] + got[half, p, r]) + zgot[p, r]
-
-    each(0, TURNS, last_step)
+            mine[p, r] = term[core, half, p, r] + got[half, p, r]
+
+    each(0, TURNS, own_sums)
+    keep = pltpu.make_async_copy(mine, mine_hbm, load_sem.at[0])
+    keep.start()
+    each(0, TURNS, lambda r: to_far(r).wait_recv())
+    keep.wait()
 
     def sent(k):
         for copy in (*one(k), *two(k)):
@@ -300,15 +303,15 @@
     whole = pltpu.VMEM(grid, jnp.float32)
     quarter = (planes, TURNS, *tile)
     dma = pltpu.SemaphoreType.DMA
-    out = pl.pallas_call(
+    mine, others = pl.pallas_call(
         kernel,
-        out_shape=jax.ShapeDtypeStruct(quarter, jnp.float32),
+        out_shape=[jax.ShapeDtypeStruct(quarter, jnp.float32)] * 2,
         in_specs=[
             pl.BlockSpec(memory_space=pltpu.SMEM),
             pl.BlockSpec(memory_space=pl.ANY),
             pl.BlockSpec(memory_space=pl.ANY),
         ],
-        out_specs=pl.BlockSpec(memory_space=pltpu.VMEM),
+        out_specs=[pl.BlockSpec(memory_space=pl.ANY)] * 2,
         scratch_shapes=[
             whole, whole, whole, halos, halos,
             pltpu.VMEM((2, 2, *quarter), jnp.float32),
@@ -323,7 +326,7 @@
         compiler_params=pltpu.CompilerParams(collective_id=0, has_side_effects=True),
         name="filter_density",
     )(coeffs, orbitals.reshape(grid), potential.reshape(grid))
-    return out.reshape(planes, rows // 4, width)
+    return ((mine + others) * 0.25).reshape(planes, rows // 4, width)
 
 
 def solution(mesh):

time: 92.9 us -> 91.2 us (0.982)
  other arithmetic: 0 us -> 2.08 us
  Pallas kernels: 90.8 us -> 88.8 us
  local copies, waits for them, and re-layouts: 1.87 us -> 0 us
    reshape x0 -> x1, other arithmetic: none -> 2.08 us  [shards(): return ((mine + others) * 0.25).reshape(planes, rows // 4, width)]
    pallas_call x1, Pallas kernels: 90.8 us -> 88.8 us  [shards(): pl.pallas_call(kernel, out_shape=[jax.ShapeDtypeStruct(quarter, jnp.float...]
    unnamed x1 -> x0, local copies, waits for them, and re-layouts: 1.87 us -> none
where the time goes in v5:
time: 91.2 us; the launch traced here: 90.9 us
  Pallas kernels  88.8 us (97%)
  other arithmetic  2.08 us (2%)
    pallas_call x1, Pallas kernels, shards(): pl.pallas_call(kernel, out_shape=[jax.ShapeDtypeStruct(quarter, jnp.float...  88.8 us
    reshape x1, other arithmetic, shards(): return ((mine + others) * 0.25).reshape(planes, rows // 4, width)  2.08 us

profile of v5, /device:TPU:1, one launch (start us, length us, event | category | flops | bytes accessed | tf_op | source)
XLA Modules:
  0.0 90.9 jit_solution(1288388859406667175)
XLA Ops:
  0.0 88.8 %filter_density.1 = (f32[4,8,8,512]{3,2,1,0:T(8,128)}, f32[4,8,8,512]{3,2,1,0:T(8,128)}) custom-call(f32[3]{0:T(128)} %coef.1, f32[4,2,16,8,512]{4,3,2,1,0:T(8,128)} %bitcast.4, f32[4,2,16,8,512]{4,3,2,1,0:T(8,128)} %bitcast.5), custom_call_target="tpu_custom_call" | custom-call | tf_op jit(solution)/shard_map/filter_density/pallas_call | solution.py:306
  88.8 2.1 %multiply_bitcast_fusion = f32[4,64,512]{2,1,0:T(8,128)} fusion(f32[4,8,8,512]{3,2,1,0:T(8,128)} %get-tuple-element.7, f32[4,8,8,512]{3,2,1,0:T(8,128)} %get-tuple-element.8), kind=kLoop, calls=%fused_computation | loop fusion | flops 262144 | bytes 1572864 | tf_op jit(solution)/shard_map/reshape | solution.py:329

commit v6 on v5

--- a/solution.py
+++ b/solution.py
@@ -199,9 +199,8 @@
             def _():
                 to_far(r).start()
 
-    def pass_on():
-        to_pass(pass_row, turn).wait_recv()
-        copy = pltpu.make_async_remote_copy(
+    def passed():
+        return pltpu.make_async_remote_copy(
             src_ref=passing,
             dst_ref=zgot.at[:, pass_row],
             send_sem=pass_out.at[0],
@@ -209,8 +208,10 @@
             device_id={"slab": edge, "orb": lax.rem(o + 2, 4)},
             device_id_type=MESH,
         )
-        copy.start()
-        copy.wait_send()
+
+    def pass_on():
+        to_pass(pass_row, turn).wait_recv()
+        passed().start()
 
     def each(first_k, last_k, body):
         def step(k, carry):
@@ -293,6 +294,10 @@
         to_far(r).wait_send()
 
     each(0, TURNS, sums_sent)
+
+    @pl.when(turn >= DIRECT)
+    def _():
+        passed().wait_send()
 
 
 def shards(orbitals, potential, coeffs):

time: 91.2 us -> 92.8 us (1.018); the launches traced: 90.9 us -> 91.1 us
  no operation moved by 1% of the time
where the time goes in v6:
time: 92.8 us; the launch traced here: 91.1 us
  Pallas kernels  89 us (96%)
  other arithmetic  2.08 us (2%)
    pallas_call x1, Pallas kernels, shards(): pl.pallas_call(kernel, out_shape=[jax.ShapeDtypeStruct(quarter, jnp.float...  89 us
    reshape x1, other arithmetic, shards(): return ((mine + others) * 0.25).reshape(planes, rows // 4, width)  2.08 us

profile of v6, /device:TPU:1, one launch (start us, length us, event | category | flops | bytes accessed | tf_op | source)
XLA Modules:
  0.0 91.1 jit_solution(4372039534123611320)
XLA Ops:
  0.0 89.0 %filter_density.1 = (f32[4,8,8,512]{3,2,1,0:T(8,128)}, f32[4,8,8,512]{3,2,1,0:T(8,128)}) custom-call(f32[3]{0:T(128)} %coef.1, f32[4,2,16,8,512]{4,3,2,1,0:T(8,128)} %bitcast.4, f32[4,2,16,8,512]{4,3,2,1,0:T(8,128)} %bitcast.5), custom_call_target="tpu_custom_call" | custom-call | tf_op jit(solution)/shard_map/filter_density/pallas_call | solution.py:311
  89.0 2.1 %multiply_bitcast_fusion = f32[4,64,512]{2,1,0:T(8,128)} fusion(f32[4,8,8,512]{3,2,1,0:T(8,128)} %get-tuple-element.7, f32[4,8,8,512]{3,2,1,0:T(8,128)} %get-tuple-element.8), kind=kLoop, calls=%fused_computation | loop fusion | flops 262144 | bytes 1572864 | tf_op jit(solution)/shard_map/reshape | solution.py:334
